TPU v7x, 32 devices: a whole 2x2x4 slice. The times are simulated.
32 devices in a mesh: pb: 4 (over y, core), kv: 8 (over z, x).
Axes of the slice: x: 2, y: 2, z: 4, core: 2. Of those that a mesh axis runs over, the one named last changes fastest.
Arguments:
- queries: bfloat16 [8192, 128], P(('pb', 'kv')), may hold values from -15 to 15
- query_tangent: bfloat16 [8192, 128], P(('pb', 'kv')), may hold values from -2 to 2
- keys: bfloat16 [8192, 128], P(('pb', 'kv')), may hold values from -8 to 8
- values: bfloat16 [8192, 128], P(('pb', 'kv')), may hold values from -6 to 6
- key_tangent: bfloat16 [8192, 128], P(('pb', 'kv')), may hold values from -2 to 2
- value_tangent: bfloat16 [8192, 128], P(('pb', 'kv')), may hold values from -6 to 6
- block_list: int32 [64, 8, 8], P('pb', 'kv'), may hold values from 0 to 63, as said below
- block_count: int32 [64, 8], P('pb', 'kv'), may hold values from 1 to 8, as said below
Outputs:
- attended: bfloat16 [8192, 128], P(('pb', 'kv'))
- attended_tangent: bfloat16 [8192, 128], P(('pb', 'kv'))
Inputs may be any that keep to these rules, and one draw needn't show every extreme that they name: `block_list`: entries for one query block and slab j are distinct key blocks g whose index g // (256 // 128) leaves remainder j when divided by 8; entries past block_count are valid but unused. `block_count`: the value 8 is reached in every key slab.
All inputs are finite; a program needn't handle non-finite values.
Results may differ from a plain program's by a relative error of at most 0.01.
Values may be sent and summed in bfloat16 or wider, within the bound.
A program may use at most 128 MiB of HBM per device.

v0:
```python
import math

import jax
import jax.numpy as jnp
from jax import lax
from jax.sharding import PartitionSpec as P

BLK = 128
LMAX = 8


def shards(
    queries, query_tangent, keys, values, key_tangent, value_tangent, block_list, block_count
):
    head_dim = queries.shape[1]
    shard_rows = keys.shape[0]
    shard_blocks = shard_rows // BLK
    slab_count = lax.axis_size("kv")
    score_scale = 1.0 / math.sqrt(head_dim)
    query_all, qtangent_all = (
        lax.all_gather(queries, "kv", axis=0, tiled=True),
        lax.all_gather(query_tangent, "kv", axis=0, tiled=True),
    )
    key_all, value_all, ktangent_all, vtangent_all = (
        lax.all_gather(keys, "pb", axis=0, tiled=True),
        lax.all_gather(values, "pb", axis=0, tiled=True),
        lax.all_gather(key_tangent, "pb", axis=0, tiled=True),
        lax.all_gather(value_tangent, "pb", axis=0, tiled=True),
    )
    key_blocks = key_all.reshape(-1, BLK, head_dim)
    value_blocks = value_all.reshape(-1, BLK, head_dim)
    keyt_blocks = ktangent_all.reshape(-1, BLK, head_dim)
    valuet_blocks = vtangent_all.reshape(-1, BLK, head_dim)
    global_ids = block_list[:, 0, :]
    shard_id = global_ids // shard_blocks
    local_index = shard_id // slab_count * shard_blocks + global_ids % shard_blocks
    counts_all = block_count[:, 0]
    query_blocks = query_all.shape[0] // BLK
    group_size = 8
    groups = query_blocks // group_size

    def attend(items):
        query_group, tangent_group, picked, counts = items
        flat = picked.reshape(-1)
        key_rows = key_blocks[flat].reshape(group_size, -1, head_dim)
        value_rows = value_blocks[flat].reshape(group_size, -1, head_dim)
        keyt_rows = keyt_blocks[flat].reshape(group_size, -1, head_dim)
        valuet_rows = valuet_blocks[flat].reshape(group_size, -1, head_dim)
        active = jnp.repeat(jnp.arange(LMAX)[None, :] < counts[:, None], BLK, axis=1)
        scores = (
            jnp.einsum("gqd,gkd->gqk", query_group, key_rows, preferred_element_type=jnp.float32)
            * score_scale
        )
        score_tangent = (
            jnp.einsum("gqd,gkd->gqk", tangent_group, key_rows, preferred_element_type=jnp.float32)
            + jnp.einsum("gqd,gkd->gqk", query_group, keyt_rows, preferred_element_type=jnp.float32)
        ) * score_scale
        peak = jnp.max(jnp.where(active[:, None, :], scores, -jnp.inf), axis=2)
        weights = jnp.where(active[:, None, :], jnp.exp(scores - peak[:, :, None]), 0.0)
        total = jnp.sum(weights, axis=2)
        slope = jnp.sum(weights * score_tangent, axis=2)
        weights_b = weights.astype(jnp.bfloat16)
        scaled_b = (weights * score_tangent).astype(jnp.bfloat16)
        weighted = jnp.einsum(
            "gqk,gkd->gqd", weights_b, value_rows, preferred_element_type=jnp.float32
        )
        tangent_sum = jnp.einsum(
            "gqk,gkd->gqd", scaled_b, value_rows, preferred_element_type=jnp.float32
        ) + jnp.einsum("gqk,gkd->gqd", weights_b, valuet_rows, preferred_element_type=jnp.float32)
        return (peak, total, weighted, slope, tangent_sum)

    peak, total, weighted, slope, tangent_sum = lax.map(
        attend,
        (
            query_all.reshape(groups, group_size, BLK, head_dim),
            qtangent_all.reshape(groups, group_size, BLK, head_dim),
            local_index.reshape(groups, group_size, LMAX),
            counts_all.reshape(groups, group_size),
        ),
    )
    slab_rows = query_all.shape[0]
    peak = peak.reshape(slab_rows)
    total = total.reshape(slab_rows)
    slope = slope.reshape(slab_rows)
    weighted = weighted.reshape(slab_rows, head_dim)
    tangent_sum = tangent_sum.reshape(slab_rows, head_dim)
    peak_all = lax.pmax(peak, "kv")
    factor = jnp.exp(peak - peak_all)
    total_own, weighted_own, slope_own, tangent_own = (
        lax.psum_scatter(total * factor, "kv", scatter_dimension=0, tiled=True),
        lax.psum_scatter(weighted * factor[:, None], "kv", scatter_dimension=0, tiled=True),
        lax.psum_scatter(slope * factor, "kv", scatter_dimension=0, tiled=True),
        lax.psum_scatter(tangent_sum * factor[:, None], "kv", scatter_dimension=0, tiled=True),
    )
    output = weighted_own / total_own[:, None]
    output_tangent = tangent_own / total_own[:, None] - (slope_own / total_own)[:, None] * output
    return (output.astype(jnp.bfloat16), output_tangent.astype(jnp.bfloat16))


def solution(mesh):
    in_specs = (
        P(("pb", "kv"), None),
        P(("pb", "kv"), None),
        P(("pb", "kv"), None),
        P(("pb", "kv"), None),
        P(("pb", "kv"), None),
        P(("pb", "kv"), None),
        P("pb", "kv", None),
        P("pb", "kv"),
    )
    out_specs = (P(("pb", "kv"), None), P(("pb", "kv"), None))
    return jax.shard_map(shards, mesh=mesh, in_specs=in_specs, out_specs=out_specs, check_vma=False)
```

profile of v0, /device:TPU:0, one launch (start us, length us, event | category | flops | bytes accessed | tf_op | source)
XLA Modules:
  0.0 322.6 jit_solution(14211954801585777682)
XLA Ops:
  9.2 35.4 %all_gather.18 = bf16[2048,128]{1,0:T(8,128)(2,1)} all-gather(bf16[256,128]{1,0:T(8,128)(2,1)} %param.10), channel_id=1, replica_groups=mesh['pb'=4,'kv'=8] {'kv'}, dimensions={0}, use_global_device_ids=true | all-gather | bytes 589824 | tf_op jit(solution)/shard_map/all_gather | solution.py:21
  44.6 33.6 %all_gather.21 = bf16[2048,128]{1,0:T(8,128)(2,1)} all-gather(bf16[256,128]{1,0:T(8,128)(2,1)} %param.11), channel_id=1, replica_groups=mesh['pb'=4,'kv'=8] {'kv'}, dimensions={0}, use_global_device_ids=true | all-gather | bytes 589824 | tf_op jit(solution)/shard_map/all_gather | solution.py:22
  78.2 6.0 %all_gather.19 = bf16[1024,128]{1,0:T(8,128)(2,1)S(1)} all-gather(bf16[256,128]{1,0:T(8,128)(2,1)} %param.12), channel_id=1, replica_groups=mesh['pb'=4,'kv'=8] {'pb'}, dimensions={0}, use_global_device_ids=true | all-gather | bytes 327680 | tf_op jit(solution)/shard_map/all_gather | solution.py:25
  84.2 6.0 %all_gather.20 = bf16[1024,128]{1,0:T(8,128)(2,1)S(1)} all-gather(bf16[256,128]{1,0:T(8,128)(2,1)} %param.13), channel_id=1, replica_groups=mesh['pb'=4,'kv'=8] {'pb'}, dimensions={0}, use_global_device_ids=true | all-gather | bytes 327680 | tf_op jit(solution)/shard_map/all_gather | solution.py:26
  90.2 6.0 %all_gather.22 = bf16[1024,128]{1,0:T(8,128)(2,1)S(1)} all-gather(bf16[256,128]{1,0:T(8,128)(2,1)} %param.14), channel_id=1, replica_groups=mesh['pb'=4,'kv'=8] {'pb'}, dimensions={0}, use_global_device_ids=true | all-gather | bytes 327680 | tf_op jit(solution)/shard_map/all_gather | solution.py:27
  96.3 6.0 %all_gather.23 = bf16[1024,128]{1,0:T(8,128)(2,1)S(1)} all-gather(bf16[256,128]{1,0:T(8,128)(2,1)} %param.15), channel_id=1, replica_groups=mesh['pb'=4,'kv'=8] {'pb'}, dimensions={0}, use_global_device_ids=true | all-gather | bytes 327680 | tf_op jit(solution)/shard_map/all_gather | solution.py:28
  103.2 57.1 %while.18 = (s32[]{:T(128)}, f32[2,8,128]{2,1,0:T(8,128)S(1)}, f32[2,8,128]{2,1,0:T(8,128)S(1)}, f32[2,8,128,128]{3,2,1,0:T(8,128)}, f32[2,8,128]{2,1,0:T(8,128)...) while((s32[]{:T(128)}, f32[2,8,128]{2,1,0:T(8,128)S(1)}, ...), condition=%wide.region_4.5_spmd, body=%wide.region_0.4_spmd.sunk | while | flops 1634859264 | bytes 101561608 | solution.py:72
  104.4 3.6 %select_reduce_fusion.2 = (f32[8,128]{1,0:T(8,128)S(1)}, f32[8,128,1024]{2,1,0:T(8,128)}) fusion(pred[8,1024]{1,0:T(8,128)(4,1)S(1)} %broadcast_bitcast_fusion.2, bf16[8,1024,128]{2,1,0:T(8,128)(2,1)S(1)} %bitcast.106, bf16[2,8,128,128]{3,2,1,0:T(8,128)(2,1)} %get-tuple-element.291, s32[]{:T(128)} %get-tuple-element.269), kind=kOutput, calls=%fused_computation.6.clone.1 | convolution fusion | flops 271580160 | bytes 6566400 | tf_op jit(solution)/shard_map/while/body/eval_jaxpr/gqd,gkd->gqk/dot_general | solution.py:51
  108.1 2.7 fusion.66
  110.7 2.2 gather_fusion.1
  112.9 5.8 %fusion.67 = (f32[8,128]{1,0:T(8,128)S(1)}, bf16[8,128,1024]{2,1,0:T(8,128)(2,1)S(1)}) fusion(f32[8,128,1024]{2,1,0:T(8,128)} %fusion.66, bf16[8,1024,128]{2,1,0:T(8,128)(2,1)} %bitcast.112, bf16[2,8,128,128]{3,2,1,0:T(8,128)(2,1)} %get-tuple-element.291, s32[]{:T(128)} %get-tuple-element.269, f32[8,128]{1,0:T(8,128)S(1)} %get-tuple-element.248, ...), kind=kOutput, calls=%fused_computation.61.clone.1 | convolution fusion | flops 276823040 | bytes 12861952 | tf_op jit(solution)/shard_map/while/body/eval_jaxpr/gqd,gkd->gqk/dot_general | solution.py:56
  120.8 3.1 fusion.70
  124.9 4.3 %fusion.71 = f32[2,8,128,128]{3,2,1,0:T(8,128)} fusion(f32[2,8,128,128]{3,2,1,0:T(8,128)} %get-tuple-element.274, s32[]{:T(128)} %get-tuple-element.269, f32[8,128,128]{2,1,0:T(8,128)} %fusion.70, bf16[8,1024,128]{2,1,0:T(8,128)(2,1)S(1)} %bitcast.115, f32[8,128,1024]{2,1,0:T(8,128)} %get-tuple-element.249, f32[8,128]{1,0:T(8,128)S(1)} %get-tuple-element.248, ...), kind=kOutput, calls=%fused_computation.15.clone.1 | convolution fusion | flops 272760832 | bytes 7352832 | tf_op jit(solution)/shard_map/while/body/eval_jaxpr/gqk,gkd->gqd/dot_general | solution.py:69
  133.0 3.6 %select_reduce_fusion.2 = (f32[8,128]{1,0:T(8,128)S(1)}, f32[8,128,1024]{2,1,0:T(8,128)}) fusion(pred[8,1024]{1,0:T(8,128)(4,1)S(1)} %broadcast_bitcast_fusion.2, bf16[8,1024,128]{2,1,0:T(8,128)(2,1)S(1)} %bitcast.106, bf16[2,8,128,128]{3,2,1,0:T(8,128)(2,1)} %get-tuple-element.291, s32[]{:T(128)} %get-tuple-element.269), kind=kOutput, calls=%fused_computation.6.clone.1 | convolution fusion | flops 271580160 | bytes 6566400 | tf_op jit(solution)/shard_map/while/body/eval_jaxpr/gqd,gkd->gqk/dot_general | solution.py:51
  136.6 2.7 fusion.66
  139.3 2.2 gather_fusion.1
  141.5 5.7 %fusion.67 = (f32[8,128]{1,0:T(8,128)S(1)}, bf16[8,128,1024]{2,1,0:T(8,128)(2,1)S(1)}) fusion(f32[8,128,1024]{2,1,0:T(8,128)} %fusion.66, bf16[8,1024,128]{2,1,0:T(8,128)(2,1)} %bitcast.112, bf16[2,8,128,128]{3,2,1,0:T(8,128)(2,1)} %get-tuple-element.291, s32[]{:T(128)} %get-tuple-element.269, f32[8,128]{1,0:T(8,128)S(1)} %get-tuple-element.248, ...), kind=kOutput, calls=%fused_computation.61.clone.1 | convolution fusion | flops 276823040 | bytes 12861952 | tf_op jit(solution)/shard_map/while/body/eval_jaxpr/gqd,gkd->gqk/dot_general | solution.py:56
  149.4 3.1 fusion.70
  153.5 4.3 %fusion.71 = f32[2,8,128,128]{3,2,1,0:T(8,128)} fusion(f32[2,8,128,128]{3,2,1,0:T(8,128)} %get-tuple-element.274, s32[]{:T(128)} %get-tuple-element.269, f32[8,128,128]{2,1,0:T(8,128)} %fusion.70, bf16[8,1024,128]{2,1,0:T(8,128)(2,1)S(1)} %bitcast.115, f32[8,128,1024]{2,1,0:T(8,128)} %get-tuple-element.249, f32[8,128]{1,0:T(8,128)S(1)} %get-tuple-element.248, ...), kind=kOutput, calls=%fused_computation.15.clone.1 | convolution fusion | flops 272760832 | bytes 7352832 | tf_op jit(solution)/shard_map/while/body/eval_jaxpr/gqk,gkd->gqd/dot_general | solution.py:69
  160.3 21.9 %pmax.7 = f32[2048]{0:T(1024)S(1)} all-reduce(f32[2048]{0:T(1024)S(1)} %bitcast.118), channel_id=1, replica_groups=mesh['pb'=4,'kv'=8] {'kv'}, use_global_device_ids=true, to_apply=%region_5.6 | all-reduce | flops 2048 | bytes 16384 | tf_op jit(solution)/shard_map/pmax | solution.py:87
  182.3 3.2 %bitcast_multiply_fusion = (f32[2048,128]{1,0:T(8,128)}, f32[2048,128]{1,0:T(8,128)}) fusion(f32[2,8,128,128]{3,2,1,0:T(8,128)} %get-tuple-element.81, f32[2048]{0:T(1024)S(1)} %get-tuple-element.144, f32[2,8,128,128]{3,2,1,0:T(8,128)} %get-tuple-element.78), kind=kLoop, calls=%fused_computation.42 | loop fusion | flops 524288 | bytes 4202496 | tf_op jit(solution)/shard_map/mul | solution.py:93
  187.5 33.1 %all-reduce.2 = (f32[2048]{0:T(1024)S(1)}, f32[2048]{0:T(1024)S(1)}) all-reduce(f32[2048]{0:T(1024)S(1)} %bitcast_multiply_fusion.3, f32[2048]{0:T(1024)S(1)} %get-tuple-element.143), channel_id=3, replica_groups=mesh['pb'=4,'kv'=8] {'kv'}, use_global_device_ids=true, to_apply=%region_7.8.clone | all-reduce | flops 4096 | bytes 32768
  220.7 26.4 %reduce-scatter.3.cloned.1.call-done = f32[256,128]{1,0:T(8,128)} async-done(((f32[2048,128]{1,0:T(8,128)}), f32[256,128]{1,0:T(8,128)}) %reduce-scatter.3.cloned.1.call-update) | async-done | bytes 131088 | tf_op jit(solution)/shard_map/reduce_scatter | solution.py:91
  247.1 66.9 %reduce-scatter.5.cloned.1.call-done = f32[256,128]{1,0:T(8,128)} async-done(((f32[2048,128]{1,0:T(8,128)}), f32[256,128]{1,0:T(8,128)}) %reduce-scatter.5.cloned.1.call-update) | async-done | bytes 131088 | tf_op jit(solution)/shard_map/reduce_scatter | solution.py:93
  (71 shorter events, 19.6 us)
Async XLA Ops:
  7.2 239.9 %reduce-scatter.3.cloned.1.call-start = ((), (), s32[]{:S(2)}) async-start(), calls=%async_computation.2 | async-start | bytes 1179648 | tf_op jit(solution)/shard_map/reduce_scatter | solution.py:91
  104.3 3.7 %copy-start.2 = (bf16[2,8,128,128]{3,2,1,0:T(8,128)(2,1)S(1)}, bf16[2,8,128,128]{3,2,1,0:T(8,128)(2,1)}, u32[]{:S(2)}) copy-start(bf16[2,8,128,128]{3,2,1,0:T(8,128)(2,1)} %get-tuple-element.295) | copy-start | bytes 1572868 | tf_op jit(solution)/shard_map/while
  124.9 4.3 %copy-start = (f32[8,128,1024]{2,1,0:T(8,128)S(1)}, f32[8,128,1024]{2,1,0:T(8,128)}, u32[]{:S(2)}) copy-start(f32[8,128,1024]{2,1,0:T(8,128)} %get-tuple-element.249) | copy-start | bytes 12582916 | tf_op jit(solution)/shard_map/while
  124.9 4.3 %copy-start.1 = (bf16[64,128,128]{2,1,0:T(8,128)(2,1)S(1)}, bf16[64,128,128]{2,1,0:T(8,128)(2,1)}, u32[]{:S(2)}) copy-start(bf16[64,128,128]{2,1,0:T(8,128)(2,1)} %gather_fusion.2) | copy-start | bytes 6291460 | tf_op jit(solution)/shard_map/while
  124.9 4.7 %copy-start.3 = (f32[2,8,128,128]{3,2,1,0:T(8,128)S(1)}, f32[2,8,128,128]{3,2,1,0:T(8,128)}, u32[]{:S(2)}) copy-start(f32[2,8,128,128]{3,2,1,0:T(8,128)} %get-tuple-element.272) | copy-start | bytes 3145732 | tf_op jit(solution)/shard_map/while
  130.6 1.1 copy-start.4
  132.9 3.7 %copy-start.2 = (bf16[2,8,128,128]{3,2,1,0:T(8,128)(2,1)S(1)}, bf16[2,8,128,128]{3,2,1,0:T(8,128)(2,1)}, u32[]{:S(2)}) copy-start(bf16[2,8,128,128]{3,2,1,0:T(8,128)(2,1)} %get-tuple-element.295) | copy-start | bytes 1572868 | tf_op jit(solution)/shard_map/while
  153.5 4.3 %copy-start = (f32[8,128,1024]{2,1,0:T(8,128)S(1)}, f32[8,128,1024]{2,1,0:T(8,128)}, u32[]{:S(2)}) copy-start(f32[8,128,1024]{2,1,0:T(8,128)} %get-tuple-element.249) | copy-start | bytes 12582916 | tf_op jit(solution)/shard_map/while
  153.5 4.3 %copy-start.1 = (bf16[64,128,128]{2,1,0:T(8,128)(2,1)S(1)}, bf16[64,128,128]{2,1,0:T(8,128)(2,1)}, u32[]{:S(2)}) copy-start(bf16[64,128,128]{2,1,0:T(8,128)(2,1)} %gather_fusion.2) | copy-start | bytes 6291460 | tf_op jit(solution)/shard_map/while
  153.5 4.7 %copy-start.3 = (f32[2,8,128,128]{3,2,1,0:T(8,128)S(1)}, f32[2,8,128,128]{3,2,1,0:T(8,128)}, u32[]{:S(2)}) copy-start(f32[2,8,128,128]{3,2,1,0:T(8,128)} %get-tuple-element.272) | copy-start | bytes 3145732 | tf_op jit(solution)/shard_map/while
  159.1 1.1 copy-start.4
  160.3 26.0 %copy-start.5 = (u32[32]{0:T(128)S(1)}, u32[32]{0:T(128)}, u32[]{:S(2)}) copy-start(u32[32]{0:T(128)} %constant.74) | copy-start | bytes 388
  185.5 128.5 %reduce-scatter.5.cloned.1.call-start = ((), (), s32[]{:S(2)}) async-start(), calls=%async_computation.3 | async-start | bytes 1179648 | tf_op jit(solution)/shard_map/reduce_scatter | solution.py:93
Sparse Core Ops, SparseCore 0:
  185.6 61.3 reduce-scatter.2
  250.5 63.4 reduce-scatter.4
where the time goes:
time: 323 us
  blocking collectives  148 us (46%)
  waiting for transfers between devices  94 us (29%)
  matrix products  40.8 us (13%)
  local copies, waits for them, and re-layouts  15.8 us (5%)
  between operations  14.8 us (5%)
  other arithmetic  8.65 us (3%)
    reduce_scatter x1, waiting for transfers between devices, shards(): lax.psum_scatter(tangent_sum * factor[:, None], 'kv', scatter_dimension=0...  66.9 us
    all_gather x1, blocking collectives, shards(): lax.all_gather(queries, 'kv', axis=0, tiled=True)  35.4 us
    all_gather x1, blocking collectives, shards(): lax.all_gather(query_tangent, 'kv', axis=0, tiled=True)  33.6 us
    unnamed x1, blocking collectives  33.1 us
    reduce_scatter x1, waiting for transfers between devices, shards(): lax.psum_scatter(weighted * factor[:, None], 'kv', scatter_dimension=0, t...  26.4 us
    pmax x1, blocking collectives, shards(): peak_all = lax.pmax(peak, 'kv')  21.9 us
    dot_general x2, matrix products, attend(): jnp.einsum('gqd,gkd->gqk', query_group, keyt_rows, preferred_element_type...  11.5 us
    dot_general x2, matrix products, attend(): jnp.einsum('gqk,gkd->gqd', weights_b, valuet_rows, preferred_element_type...  8.55 us
  transfers between devices with their start and end apart: 2, of which 2 were waited for; matrix products, arithmetic and copies ran while one was open for 0% of the time, Pallas kernels for 0%

commit v1 on v0

v1 whole, which is shorter than its diff:
```python
import functools
import math

import jax
import jax.numpy as jnp
from jax import lax
from jax.experimental import pallas as pl
from jax.experimental.pallas import tpu as pltpu
from jax.sharding import PartitionSpec as P

BLK = 128
NT = (((1,), (1,)), ((), ()))
MESH = pl.DeviceIdType.MESH


def flip(a, b, bits):
    out = 0
    for k in range(bits):
        w = 1 << k
        out = out + (a // w + b // w) % 2 * w
    return out


def kernel(
    zc, q_in, qt_in, k_in, v_in, kt_in, vt_in, bias_in, out_ref, outt_ref,
    kv, qq, bias_x, s_scr, p_scr, ps_scr, send, sstat, recv, rstat, coef,
    local_sem, ks, kr, qs, qr, bs, rs, rr, ts, tr,
):
    rows, hd = q_in.shape
    half = rows // 2
    bits = zc.bit_length() - 1
    scale = 1.0 / math.sqrt(hd)
    factor = scale * math.log2(math.e)
    pb, kvi = lax.axis_index("pb"), lax.axis_index("kv")
    y, c, z, x = pb // 2, pb % 2, kvi // 2, kvi % 2
    to_x = (pb, kvi + 1 - 2 * x)
    to_y = (pb + 2 - 4 * y, kvi)
    to_c = (pb + 1 - 2 * c, kvi)

    def to_z(mask):
        return (pb, flip(z, mask, bits) * 2 + x)

    loads = []
    for n, (src, dst) in enumerate(
        [
            (k_in, kv.at[0, :, pl.ds(0, hd)]),
            (kt_in, kv.at[0, :, pl.ds(hd, hd)]),
            (v_in, kv.at[0, :, pl.ds(2 * hd, hd)]),
            (vt_in, kv.at[0, :, pl.ds(3 * hd, hd)]),
            (qt_in, qq.at[0, :, pl.ds(0, hd)]),
            (q_in, qq.at[0, :, pl.ds(hd, hd)]),
        ]
    ):
        copy = pltpu.make_async_copy(src, dst, local_sem.at[n])
        copy.start()
        loads.append(copy)

    barrier = pltpu.get_barrier_semaphore()
    for dev in [to_x, to_y, to_c] + [to_z(m) for m in range(1, zc)]:
        pl.semaphore_signal(barrier, inc=1, device_id=dev, device_id_type=MESH)
    pl.semaphore_wait(barrier, 2 + zc)
    for copy in loads:
        copy.wait()

    def remote(src, dst, ssem, rsem, dev):
        return pltpu.make_async_remote_copy(
            src_ref=src, dst_ref=dst, send_sem=ssem, recv_sem=rsem,
            device_id=dev, device_id_type=MESH,
        )

    sent = []

    def piece(slot, h):
        return kv.at[slot, pl.ds(h * half, half)]

    def give(slot, h, dst, dev):
        copy = remote(piece(slot, h), piece(dst, h), ks.at[dst, h], kr.at[dst, h], dev)
        copy.start()
        sent.append(copy)

    def got(slot, h):
        remote(piece(slot, h), piece(slot, h), ks.at[slot, h], kr.at[slot, h], to_c).wait_recv()

    give(0, 1, 1, to_x)
    give(0, 0, 2, to_y)
    give(0, 0, 1, to_x)
    give(0, 1, 2, to_y)
    for m in range(zc - 1, 0, -1):
        copy = remote(qq.at[0], qq.at[m], qs.at[m], qr.at[m], to_z(m))
        copy.start()
        sent.append(copy)
    give(0, 0, 4, to_c)
    give(0, 1, 4, to_c)
    bias_copy = remote(bias_in.at[1 - x], bias_x, bs.at[0], bs.at[1], to_x)
    bias_copy.start()
    got(2, 0)
    give(2, 0, 3, to_x)
    give(2, 0, 6, to_c)
    got(1, 1)
    give(1, 1, 3, to_y)
    give(1, 1, 5, to_c)
    got(1, 0)
    give(1, 0, 5, to_c)
    got(2, 1)
    give(2, 1, 6, to_c)
    got(3, 0)
    give(3, 0, 7, to_c)
    got(3, 1)
    give(3, 1, 7, to_c)
    bias_copy.wait_recv()
    for slot in range(4, 8):
        for h in range(2):
            got(slot, h)

    def attend(mask):
        zt = flip(z, mask, bits)
        best = None
        for r in range(8):
            pbr = flip(pb, (r // 2) % 2 * 2 + r // 4, 2)
            if r % 2 == 0:
                b = bias_in[x, pbr, zt]
            else:
                b = bias_x[pbr, zt]
            s = lax.dot_general(
                qq[mask, :, hd:], kv[r, :, 0:hd], NT, preferred_element_type=jnp.float32
            )
            s = (s.reshape(2, half, rows) + b[:, None, :]).reshape(rows, rows)
            s_scr[:, r * rows : (r + 1) * rows] = s
            top = jnp.maximum(s[:, :hd], s[:, hd:])
            best = top if best is None else jnp.maximum(best, top)
        peak = jnp.max(best, axis=1, keepdims=True)
        total = slope = None
        for r in range(8):
            p = jnp.exp2((s_scr[:, r * rows : (r + 1) * rows] - peak) * factor)
            t = lax.dot_general(
                qq[mask], kv[r, :, 0 : 2 * hd], NT, preferred_element_type=jnp.float32
            )
            pt = p * t
            p_scr[:, r * rows : (r + 1) * rows] = p.astype(jnp.bfloat16)
            ps_scr[:, r * rows : (r + 1) * rows] = pt.astype(jnp.bfloat16)
            p2 = p[:, :hd] + p[:, hd:]
            pt2 = pt[:, :hd] + pt[:, hd:]
            total = p2 if total is None else total + p2
            slope = pt2 if slope is None else slope + pt2
        total = jnp.sum(total, axis=1, keepdims=True)
        slope = jnp.sum(slope, axis=1, keepdims=True) * scale
        both = jnp.dot(
            p_scr[...], kv[:, :, 2 * hd :].reshape(8 * rows, 2 * hd),
            preferred_element_type=jnp.float32,
        )
        tang = jnp.dot(
            ps_scr[...], kv[:, :, 2 * hd : 3 * hd].reshape(8 * rows, hd),
            preferred_element_type=jnp.float32,
        )
        weighted = both[:, :hd]
        mean = slope / total
        centred = tang * scale + both[:, hd:] - mean * weighted
        lane = lax.broadcasted_iota(jnp.int32, (rows, hd), 1)
        stats = jnp.where(lane == 0, peak, jnp.where(lane == 1, total, mean))
        return weighted, centred, stats.T[0:8]

    def result_copies(mask):
        dev = to_z(mask)
        return (
            remote(send.at[mask], recv.at[mask], rs.at[mask], rr.at[mask], dev),
            remote(sstat.at[mask], rstat.at[mask], ts.at[mask], tr.at[mask], dev),
        )

    def step(t, carry):
        mask = zc - 1 - t
        remote(qq.at[0], qq.at[mask], qs.at[mask], qr.at[mask], to_c).wait_recv()
        weighted, centred, stats = attend(mask)
        send[mask, :, 0:hd] = weighted.astype(jnp.bfloat16)
        send[mask, :, hd:] = centred.astype(jnp.bfloat16)
        sstat[mask] = stats
        for copy in result_copies(mask):
            copy.start()
        return carry

    lax.fori_loop(0, zc - 1, step, 0)
    own_w, own_c, own_stats = attend(0)
    recv[0, :, 0:hd] = own_w.astype(jnp.bfloat16)
    recv[0, :, hd:] = own_c.astype(jnp.bfloat16)
    rstat[0] = own_stats
    for m in range(1, zc):
        for copy in result_copies(m):
            copy.wait_recv()

    peaks = [rstat[m, 0:1, :] for m in range(zc)]
    peak = functools.reduce(jnp.maximum, peaks)
    shares = [jnp.exp2((pk - peak) * factor) for pk in peaks]
    total = sum(a * rstat[m, 1:2, :] for m, a in enumerate(shares))
    mean = sum(a * rstat[m, 1:2, :] * rstat[m, 2:3, :] for m, a in enumerate(shares)) / total
    coef[...] = jnp.zeros_like(coef)
    for m, a in enumerate(shares):
        a = a / total
        coef[2 * m : 2 * m + 1, :] = a
        coef[2 * m + 1 : 2 * m + 2, :] = a * (rstat[m, 2:3, :] - mean)
    columns = coef[...].T
    out = outt = 0.0
    for m in range(zc):
        w = recv[m, :, 0:hd].astype(jnp.float32)
        d = recv[m, :, hd:].astype(jnp.float32)
        a, g = columns[:, 2 * m : 2 * m + 1], columns[:, 2 * m + 1 : 2 * m + 2]
        out = out + a * w
        outt = outt + (a * d + g * w)
    out_ref[...] = out.astype(out_ref.dtype)
    outt_ref[...] = outt.astype(outt_ref.dtype)
    for copy in sent:
        copy.wait_send()
    bias_copy.wait_send()
    for m in range(1, zc):
        for copy in result_copies(m):
            copy.wait_send()


def shards(
    queries, query_tangent, keys, values, key_tangent, value_tangent, block_list, block_count
):
    rows, hd = keys.shape
    shard_blocks = rows // BLK
    slabs, pbs = lax.axis_size("kv"), lax.axis_size("pb")
    zc = slabs // 2
    slab_blocks = pbs * shard_blocks
    ids = block_list[:, 0, :]
    shard_id = ids // shard_blocks
    local = shard_id // slabs * shard_blocks + ids % shard_blocks
    used = jnp.arange(ids.shape[1])[None, :] < block_count
    on = jnp.any(
        (local[:, :, None] == jnp.arange(slab_blocks)[None, None, :]) & used[:, :, None], axis=1
    )
    on = on.reshape(zc, 2, shard_blocks, pbs, shard_blocks).transpose(1, 3, 0, 2, 4)
    on = on.reshape(2, pbs, zc, shard_blocks, shard_blocks, 1)
    bias = jnp.broadcast_to(
        jnp.where(on, 0.0, -1e30).astype(jnp.float32), on.shape[:-1] + (BLK,)
    ).reshape(2, pbs, zc, shard_blocks, rows)
    vmem = pl.BlockSpec(memory_space=pltpu.VMEM)
    hbm = pl.BlockSpec(memory_space=pl.ANY)
    dma = pltpu.SemaphoreType.DMA
    out = jax.ShapeDtypeStruct((rows, hd), jnp.bfloat16)
    return pl.pallas_call(
        functools.partial(kernel, zc),
        out_shape=(out, out),
        in_specs=[hbm] * 6 + [vmem],
        out_specs=(vmem, vmem),
        scratch_shapes=[
            pltpu.VMEM((8, rows, 4 * hd), jnp.bfloat16),
            pltpu.VMEM((zc, rows, 2 * hd), jnp.bfloat16),
            pltpu.VMEM((pbs, zc, shard_blocks, rows), jnp.float32),
            pltpu.VMEM((rows, 8 * rows), jnp.float32),
            pltpu.VMEM((rows, 8 * rows), jnp.bfloat16),
            pltpu.VMEM((rows, 8 * rows), jnp.bfloat16),
            pltpu.VMEM((zc, rows, 2 * hd), jnp.bfloat16),
            pltpu.VMEM((zc, 8, rows), jnp.float32),
            pltpu.VMEM((zc, rows, 2 * hd), jnp.bfloat16),
            pltpu.VMEM((zc, 8, rows), jnp.float32),
            pltpu.VMEM((128, rows), jnp.float32),
            dma((6,)),
            dma((8, 2)),
            dma((8, 2)),
            dma((zc,)),
            dma((zc,)),
            dma((2,)),
            dma((zc,)),
            dma((zc,)),
            dma((zc,)),
            dma((zc,)),
        ],
        compiler_params=pltpu.CompilerParams(
            collective_id=0, has_side_effects=True, vmem_limit_bytes=40 * 1024 * 1024
        ),
    )(queries, query_tangent, keys, values, key_tangent, value_tangent, bias)


def solution(mesh):
    rows = P(("pb", "kv"), None)
    return jax.shard_map(
        shards,
        mesh=mesh,
        in_specs=(rows,) * 6 + (P("pb", "kv", None), P("pb", "kv")),
        out_specs=(rows, rows),
        check_vma=False,
    )
```

time: 323 us -> 38.6 us (0.12)
  blocking collectives: 148 us -> 0 us
  waiting for transfers between devices: 94 us -> 0 us
  matrix products: 40.8 us -> 0 us
  Pallas kernels: 0 us -> 32.7 us
  between operations: 14.8 us -> 0.72 us
  local copies, waits for them, and re-layouts: 15.8 us -> 4.16 us
  other arithmetic: 8.65 us -> 0.73 us
    reduce_scatter x2 -> x0, waiting for transfers between devices: 93.3 us -> none  [the longest x1 66.9 us: shards(): lax.psum_scatter(tangent_sum * factor[:, None], 'kv', scatter_dimension=0...]
    all_gather x6 -> x0, blocking collectives: 93.2 us -> none  [the longest x1 35.4 us: shards(): lax.all_gather(queries, 'kv', axis=0, tiled=True)]
    dot_general x12 -> x0, matrix products: 40.8 us -> none  [the longest x2 11.5 us: attend(): jnp.einsum('gqd,gkd->gqk', query_group, keyt_rows, preferred_element_type...]
    unnamed x1 -> x0, blocking collectives: 33.1 us -> none
    pallas_call x0 -> x1, Pallas kernels: none -> 32.7 us  [shards(): pl.pallas_call(functools.partial(kernel, zc), out_shape=(out, out), in_sp...]
    pmax x1 -> x0, blocking collectives: 21.9 us -> none  [shards(): peak_all = lax.pmax(peak, 'kv')]
    gather x8 -> x0, local copies, waits for them, and re-layouts: 12.5 us -> none  [the longest x2 4.41 us: attend(): keyt_rows = keyt_blocks[flat].reshape(group_size, -1, head_dim)]
    mul x3 -> x0, other arithmetic: 3.25 us -> none  [the longest x1 3.23 us: shards(): tangent_sum * factor[:, None]]
  transfers between devices with their start and end apart: 2 -> 0, of which waited for: 2 -> 0; matrix products, arithmetic and copies ran while one was open for 0% -> 0% of each run, Pallas kernels for 0% -> 0%
where the time goes in v1:
time: 38.6 us; the launch traced here: 38.3 us
  Pallas kernels  32.7 us (85%)
  local copies, waits for them, and re-layouts  4.16 us (11%)
  other arithmetic  0.73 us (2%)
  between operations  0.72 us (2%)
    pallas_call x1, Pallas kernels, shards(): pl.pallas_call(functools.partial(kernel, zc), out_shape=(out, out), in_sp...  32.7 us
    unnamed x16, local copies, waits for them, and re-layouts  3.56 us

profile of v1, /device:TPU:0, one launch (start us, length us, event | category | flops | bytes accessed | tf_op | source)
XLA Modules:
  0.0 38.3 jit_solution(7943669476291512176)
XLA Ops:
  0.6 0.0 copy-start.6
  0.6 0.6 %copy-done.6 = s32[16,1]{0,1:T(1,128)S(1)} copy-done((s32[16,1]{0,1:T(1,128)S(1)}, s32[16,1]{0,1:T(1,128)}, u32[]{:S(2)}) %copy-start.6) | copy-done | bytes 88
  1.3 0.7 %fusion.4 = s32[16,8]{0,1:T(8,128)S(1)} fusion(s32[16,1,8]{0,2,1:T(8,128)} %param.14), kind=kLoop, calls=%fused_computation.14 | loop fusion | flops 4608 | bytes 1024 | tf_op jit(solution)/shard_map/add | solution.py:227
  2.0 0.0 copy-start.4
  2.0 0.1 select_n.42
  2.1 0.0 copy-start.3
  2.2 0.3 copy.14
  2.5 0.0 copy-start.2
  2.5 0.1 broadcast_in_dim.19
  2.6 0.0 copy-start
  2.6 0.0 copy-start.1
  2.6 0.1 reshape.101.bias_in
  2.7 0.2 copy-done.4
  2.9 0.1 copy-done.3
  3.0 0.3 copy-done.2
  3.3 0.1 copy-done
  3.5 0.0 copy-done.1
  3.5 0.0 copy-start.5
  3.5 0.8 %copy-done.5 = bf16[256,128]{1,0:T(8,128)(2,1)S(1)} copy-done((bf16[256,128]{1,0:T(8,128)(2,1)S(1)}, bf16[256,128]{1,0:T(8,128)(2,1)}, u32[]{:S(2)}) %copy-start.5) | copy-done | bytes 65560
  4.3 32.7 %shard_map.98 = (bf16[256,128]{1,0:T(8,128)(2,1)S(1)}, bf16[256,128]{1,0:T(8,128)(2,1)S(1)}) custom-call(bf16[256,128]{1,0:T(8,128)(2,1)S(1)} %copy-done, bf16[256,128]{1,0:T(8,128)(2,1)S(1)} %copy-done.1, bf16[256,128]{1,0:T(8,128)(2,1)S(1)} %copy-done.2, bf16[256,128]{1,0:T(8,128)(2,1)S(1)} %copy-done.3, bf16[256,128]{1,0:T(8,128)(2,1)S(1)} %copy-done.4, ...), custom_call_target="tpu_custom_call" | custom-call | tf_op jit(solution)/shard_map/pallas_call | solution.py:241
  37.1 0.6 %copy.17 = bf16[256,128]{1,0:T(8,128)(2,1)} copy(bf16[256,128]{1,0:T(8,128)(2,1)S(1)} %get-tuple-element.4) | data formatting | bytes 131072
  37.7 0.6 %copy.18 = bf16[256,128]{1,0:T(8,128)(2,1)} copy(bf16[256,128]{1,0:T(8,128)(2,1)S(1)} %get-tuple-element.5) | data formatting | bytes 131072
  (3 shorter events, 0.0 us)
Async XLA Ops:
  0.6 0.7 %copy-start.6 = (s32[16,1]{0,1:T(1,128)S(1)}, s32[16,1]{0,1:T(1,128)}, u32[]{:S(2)}) copy-start(s32[16,1]{0,1:T(1,128)} %param.15) | copy-start | bytes 196
  2.0 0.8 %copy-start.4 = (bf16[256,128]{1,0:T(8,128)(2,1)S(1)}, bf16[256,128]{1,0:T(8,128)(2,1)}, u32[]{:S(2)}) copy-start(bf16[256,128]{1,0:T(8,128)(2,1)} %kt_in.1) | copy-start | bytes 196612
  2.1 0.8 %copy-start.3 = (bf16[256,128]{1,0:T(8,128)(2,1)S(1)}, bf16[256,128]{1,0:T(8,128)(2,1)}, u32[]{:S(2)}) copy-start(bf16[256,128]{1,0:T(8,128)(2,1)} %v_in.1) | copy-start | bytes 196612
  2.5 0.9 %copy-start.2 = (bf16[256,128]{1,0:T(8,128)(2,1)S(1)}, bf16[256,128]{1,0:T(8,128)(2,1)}, u32[]{:S(2)}) copy-start(bf16[256,128]{1,0:T(8,128)(2,1)} %k_in.1) | copy-start | bytes 196612
  2.6 0.9 %copy-start = (bf16[256,128]{1,0:T(8,128)(2,1)S(1)}, bf16[256,128]{1,0:T(8,128)(2,1)}, u32[]{:S(2)}) copy-start(bf16[256,128]{1,0:T(8,128)(2,1)} %q_in.1) | copy-start | bytes 196612
  2.6 0.9 %copy-start.1 = (bf16[256,128]{1,0:T(8,128)(2,1)S(1)}, bf16[256,128]{1,0:T(8,128)(2,1)}, u32[]{:S(2)}) copy-start(bf16[256,128]{1,0:T(8,128)(2,1)} %qt_in.1) | copy-start | bytes 196612
  3.5 0.8 %copy-start.5 = (bf16[256,128]{1,0:T(8,128)(2,1)S(1)}, bf16[256,128]{1,0:T(8,128)(2,1)}, u32[]{:S(2)}) copy-start(bf16[256,128]{1,0:T(8,128)(2,1)} %vt_in.1) | copy-start | bytes 196612

commit v2 on v1

--- a/solution.py
+++ b/solution.py
@@ -22,8 +22,8 @@
 
 
 def kernel(
-    zc, q_in, qt_in, k_in, v_in, kt_in, vt_in, bias_in, out_ref, outt_ref,
-    kv, qq, bias_x, s_scr, p_scr, ps_scr, send, sstat, recv, rstat, coef,
+    zc, slabs, q_in, qt_in, k_in, v_in, kt_in, vt_in, list_in, count_in, out_ref,
+    kv, qq, lst, cnt, bias, s_scr, p_scr, ps_scr, send, sstat, recv, rstat, coef,
     local_sem, ks, kr, qs, qr, bs, rs, rr, ts, tr,
 ):
     rows, hd = q_in.shape
@@ -49,6 +49,8 @@
             (vt_in, kv.at[0, :, pl.ds(3 * hd, hd)]),
             (qt_in, qq.at[0, :, pl.ds(0, hd)]),
             (q_in, qq.at[0, :, pl.ds(hd, hd)]),
+            (list_in, lst.at[0]),
+            (count_in, cnt.at[0]),
         ]
     ):
         copy = pltpu.make_async_copy(src, dst, local_sem.at[n])
@@ -91,8 +93,39 @@
         sent.append(copy)
     give(0, 0, 4, to_c)
     give(0, 1, 4, to_c)
-    bias_copy = remote(bias_in.at[1 - x], bias_x, bs.at[0], bs.at[1], to_x)
-    bias_copy.start()
+    tables = [
+        remote(lst.at[0], lst.at[1], bs.at[0], bs.at[1], to_x),
+        remote(cnt.at[0], cnt.at[1], bs.at[2], bs.at[3], to_x),
+    ]
+    for copy in tables:
+        copy.start()
+
+    def mask_rows(side):
+        blocks = lst.shape[2]
+        shard_blocks = rows // BLK
+        slab_blocks = 4 * shard_blocks
+        ids = lst[side]
+        local = ids // (shard_blocks * slabs) * shard_blocks + ids % shard_blocks
+        used = lax.broadcasted_iota(jnp.int32, ids.shape, 0) < cnt[side]
+        row = lax.broadcasted_iota(jnp.int32, (slab_blocks, blocks), 0)
+        on = jnp.zeros((slab_blocks, blocks), jnp.float32)
+        for g in range(slab_blocks):
+            hit = jnp.max(jnp.where((local == g) & used, 1.0, 0.0), axis=0, keepdims=True)
+            on = jnp.where(row == g, hit, on)
+        spread = jnp.where(
+            lax.broadcasted_iota(jnp.int32, (slab_blocks, 4 * rows), 1) // BLK
+            == lax.broadcasted_iota(jnp.int32, (slab_blocks, 4 * rows), 0),
+            1.0, 0.0,
+        )
+        full = lax.dot_general(
+            on, spread, (((0,), (0,)), ((), ())), preferred_element_type=jnp.float32
+        )
+        full = (full - 1.0) * 1e30
+        for g in range(blocks):
+            for p in range(4):
+                bias[side, g, p] = full[g : g + 1, p * rows : (p + 1) * rows]
+
+    mask_rows(0)
     got(2, 0)
     give(2, 0, 3, to_x)
     give(2, 0, 6, to_c)
@@ -103,61 +136,71 @@
     give(1, 0, 5, to_c)
     got(2, 1)
     give(2, 1, 6, to_c)
-    got(3, 0)
-    give(3, 0, 7, to_c)
-    got(3, 1)
-    give(3, 1, 7, to_c)
-    bias_copy.wait_recv()
-    for slot in range(4, 8):
-        for h in range(2):
-            got(slot, h)
-
-    def attend(mask):
+    for copy in tables:
+        copy.wait_recv()
+    mask_rows(1)
+
+    def partial(mask, slots):
         zt = flip(z, mask, bits)
         best = None
-        for r in range(8):
+        for n, r in enumerate(slots):
             pbr = flip(pb, (r // 2) % 2 * 2 + r // 4, 2)
-            if r % 2 == 0:
-                b = bias_in[x, pbr, zt]
-            else:
-                b = bias_x[pbr, zt]
             s = lax.dot_general(
                 qq[mask, :, hd:], kv[r, :, 0:hd], NT, preferred_element_type=jnp.float32
             )
-            s = (s.reshape(2, half, rows) + b[:, None, :]).reshape(rows, rows)
-            s_scr[:, r * rows : (r + 1) * rows] = s
+            s = jnp.concatenate(
+                [
+                    s[h * half : (h + 1) * half] + bias[r % 2, (zt * 2 + x) * 2 + h, pbr]
+                    for h in range(2)
+                ],
+                axis=0,
+            )
+            s_scr[:, n * rows : (n + 1) * rows] = s
             top = jnp.maximum(s[:, :hd], s[:, hd:])
             best = top if best is None else jnp.maximum(best, top)
         peak = jnp.max(best, axis=1, keepdims=True)
         total = slope = None
-        for r in range(8):
-            p = jnp.exp2((s_scr[:, r * rows : (r + 1) * rows] - peak) * factor)
+        for n, r in enumerate(slots):
+            p = jnp.exp2((s_scr[:, n * rows : (n + 1) * rows] - peak) * factor)
             t = lax.dot_general(
                 qq[mask], kv[r, :, 0 : 2 * hd], NT, preferred_element_type=jnp.float32
             )
             pt = p * t
-            p_scr[:, r * rows : (r + 1) * rows] = p.astype(jnp.bfloat16)
-            ps_scr[:, r * rows : (r + 1) * rows] = pt.astype(jnp.bfloat16)
+            p_scr[:, n * rows : (n + 1) * rows] = p.astype(jnp.bfloat16)
+            ps_scr[:, n * rows : (n + 1) * rows] = pt.astype(jnp.bfloat16)
             p2 = p[:, :hd] + p[:, hd:]
             pt2 = pt[:, :hd] + pt[:, hd:]
             total = p2 if total is None else total + p2
             slope = pt2 if slope is None else slope + pt2
         total = jnp.sum(total, axis=1, keepdims=True)
-        slope = jnp.sum(slope, axis=1, keepdims=True) * scale
+        slope = jnp.sum(slope, axis=1, keepdims=True)
+        lo, size = slots[0], len(slots)
         both = jnp.dot(
-            p_scr[...], kv[:, :, 2 * hd :].reshape(8 * rows, 2 * hd),
+            p_scr[:, 0 : size * rows],
+            kv[lo : lo + size, :, 2 * hd :].reshape(size * rows, 2 * hd),
             preferred_element_type=jnp.float32,
         )
         tang = jnp.dot(
-            ps_scr[...], kv[:, :, 2 * hd : 3 * hd].reshape(8 * rows, hd),
+            ps_scr[:, 0 : size * rows],
+            kv[lo : lo + size, :, 2 * hd : 3 * hd].reshape(size * rows, hd),
             preferred_element_type=jnp.float32,
         )
-        weighted = both[:, :hd]
-        mean = slope / total
-        centred = tang * scale + both[:, hd:] - mean * weighted
+        return peak, total, slope, both[:, :hd], tang * scale + both[:, hd:]
+
+    def close(peak, total, slope, weighted, tang):
+        mean = slope * scale / total
+        centred = tang - mean * weighted
         lane = lax.broadcasted_iota(jnp.int32, (rows, hd), 1)
         stats = jnp.where(lane == 0, peak, jnp.where(lane == 1, total, mean))
         return weighted, centred, stats.T[0:8]
+
+    def attend(mask):
+        return close(*partial(mask, range(8)))
+
+    def join(a, b):
+        peak = jnp.maximum(a[0], b[0])
+        fa, fb = jnp.exp2((a[0] - peak) * factor), jnp.exp2((b[0] - peak) * factor)
+        return (peak,) + tuple(fa * m + fb * n for m, n in zip(a[1:], b[1:]))
 
     def result_copies(mask):
         dev = to_z(mask)
@@ -166,18 +209,37 @@
             remote(sstat.at[mask], rstat.at[mask], ts.at[mask], tr.at[mask], dev),
         )
 
-    def step(t, carry):
-        mask = zc - 1 - t
-        remote(qq.at[0], qq.at[mask], qs.at[mask], qr.at[mask], to_c).wait_recv()
-        weighted, centred, stats = attend(mask)
+    def hand_in(mask, weighted, centred, stats):
         send[mask, :, 0:hd] = weighted.astype(jnp.bfloat16)
         send[mask, :, hd:] = centred.astype(jnp.bfloat16)
         sstat[mask] = stats
         for copy in result_copies(mask):
             copy.start()
+
+    def got_queries(mask):
+        remote(qq.at[0], qq.at[mask], qs.at[mask], qr.at[mask], to_c).wait_recv()
+
+    far = zc - 1
+    got_queries(far)
+    for slot in (4, 5, 6):
+        for h in range(2):
+            got(slot, h)
+    early = join(partial(far, (0, 1, 2)), partial(far, (4, 5, 6)))
+    for h in range(2):
+        got(3, h)
+        give(3, h, 7, to_c)
+    early = join(early, partial(far, (3,)))
+    for h in range(2):
+        got(7, h)
+    hand_in(far, *close(*join(early, partial(far, (7,)))))
+
+    def step(t, carry):
+        mask = zc - 1 - t
+        got_queries(mask)
+        hand_in(mask, *attend(mask))
         return carry
 
-    lax.fori_loop(0, zc - 1, step, 0)
+    lax.fori_loop(1, zc - 1, step, 0)
     own_w, own_c, own_stats = attend(0)
     recv[0, :, 0:hd] = own_w.astype(jnp.bfloat16)
     recv[0, :, hd:] = own_c.astype(jnp.bfloat16)
@@ -204,11 +266,12 @@
         a, g = columns[:, 2 * m : 2 * m + 1], columns[:, 2 * m + 1 : 2 * m + 2]
         out = out + a * w
         outt = outt + (a * d + g * w)
-    out_ref[...] = out.astype(out_ref.dtype)
-    outt_ref[...] = outt.astype(outt_ref.dtype)
+    out_ref[:, 0:hd] = out.astype(out_ref.dtype)
+    out_ref[:, hd:] = outt.astype(out_ref.dtype)
     for copy in sent:
         copy.wait_send()
-    bias_copy.wait_send()
+    for copy in tables:
+        copy.wait_send()
     for m in range(1, zc):
         for copy in result_copies(m):
             copy.wait_send()
@@ -218,35 +281,25 @@
     queries, query_tangent, keys, values, key_tangent, value_tangent, block_list, block_count
 ):
     rows, hd = keys.shape
-    shard_blocks = rows // BLK
     slabs, pbs = lax.axis_size("kv"), lax.axis_size("pb")
     zc = slabs // 2
-    slab_blocks = pbs * shard_blocks
-    ids = block_list[:, 0, :]
-    shard_id = ids // shard_blocks
-    local = shard_id // slabs * shard_blocks + ids % shard_blocks
-    used = jnp.arange(ids.shape[1])[None, :] < block_count
-    on = jnp.any(
-        (local[:, :, None] == jnp.arange(slab_blocks)[None, None, :]) & used[:, :, None], axis=1
-    )
-    on = on.reshape(zc, 2, shard_blocks, pbs, shard_blocks).transpose(1, 3, 0, 2, 4)
-    on = on.reshape(2, pbs, zc, shard_blocks, shard_blocks, 1)
-    bias = jnp.broadcast_to(
-        jnp.where(on, 0.0, -1e30).astype(jnp.float32), on.shape[:-1] + (BLK,)
-    ).reshape(2, pbs, zc, shard_blocks, rows)
+    list_t = block_list[:, 0, :].T
+    count_t = block_count.T
+    blocks = list_t.shape[1]
     vmem = pl.BlockSpec(memory_space=pltpu.VMEM)
     hbm = pl.BlockSpec(memory_space=pl.ANY)
     dma = pltpu.SemaphoreType.DMA
-    out = jax.ShapeDtypeStruct((rows, hd), jnp.bfloat16)
-    return pl.pallas_call(
-        functools.partial(kernel, zc),
-        out_shape=(out, out),
-        in_specs=[hbm] * 6 + [vmem],
-        out_specs=(vmem, vmem),
+    out = pl.pallas_call(
+        functools.partial(kernel, zc, slabs),
+        out_shape=jax.ShapeDtypeStruct((rows, 2 * hd), jnp.bfloat16),
+        in_specs=[hbm] * 8,
+        out_specs=vmem,
         scratch_shapes=[
             pltpu.VMEM((8, rows, 4 * hd), jnp.bfloat16),
             pltpu.VMEM((zc, rows, 2 * hd), jnp.bfloat16),
-            pltpu.VMEM((pbs, zc, shard_blocks, rows), jnp.float32),
+            pltpu.VMEM((2,) + list_t.shape, jnp.int32),
+            pltpu.VMEM((2, 1, blocks), jnp.int32),
+            pltpu.VMEM((2, blocks, pbs, 1, rows), jnp.float32),
             pltpu.VMEM((rows, 8 * rows), jnp.float32),
             pltpu.VMEM((rows, 8 * rows), jnp.bfloat16),
             pltpu.VMEM((rows, 8 * rows), jnp.bfloat16),
@@ -255,21 +308,22 @@
             pltpu.VMEM((zc, rows, 2 * hd), jnp.bfloat16),
             pltpu.VMEM((zc, 8, rows), jnp.float32),
             pltpu.VMEM((128, rows), jnp.float32),
-            dma((6,)),
+            dma((8,)),
             dma((8, 2)),
             dma((8, 2)),
             dma((zc,)),
             dma((zc,)),
-            dma((2,)),
+            dma((4,)),
             dma((zc,)),
             dma((zc,)),
             dma((zc,)),
             dma((zc,)),
         ],
         compiler_params=pltpu.CompilerParams(
-            collective_id=0, has_side_effects=True, vmem_limit_bytes=40 * 1024 * 1024
+            collective_id=0, has_side_effects=True, vmem_limit_bytes=62 * 1024 * 1024
         ),
-    )(queries, query_tangent, keys, values, key_tangent, value_tangent, bias)
+    )(queries, query_tangent, keys, values, key_tangent, value_tangent, list_t, count_t)
+    return out[:, :hd], out[:, hd:]
 
 
 def solution(mesh):

time: 38.6 us -> 36 us (0.933)
  local copies, waits for them, and re-layouts: 4.16 us -> 1.53 us
  Pallas kernels: 32.7 us -> 33.7 us
  other arithmetic: 0.73 us -> 0 us
    unnamed x16 -> x0, local copies, waits for them, and re-layouts: 3.56 us -> none
    slice x0 -> x1, local copies, waits for them, and re-layouts: none -> 1.53 us  [shards(): return (out[:, :hd], out[:, hd:])]
    pallas_call x1, Pallas kernels: 32.7 us -> 33.7 us  [shards(): pl.pallas_call(functools.partial(kernel, zc, slabs), out_shape=jax.ShapeD...]
    add x1 -> x0, other arithmetic: 0.7 us -> none  [shards(): local = shard_id // slabs * shard_blocks + ids % shard_blocks]
    select_n x2 -> x0, local copies, waits for them, and re-layouts: 0.4 us -> none  [shards(): jnp.where(on, 0.0, -1e+30).astype(jnp.float32)]
where the time goes in v2:
time: 36 us; the launch traced here: 35.9 us
  Pallas kernels  33.7 us (94%)
  local copies, waits for them, and re-layouts  1.53 us (4%)
  between operations  0.64 us (2%)
    pallas_call x1, Pallas kernels, shards(): pl.pallas_call(functools.partial(kernel, zc, slabs), out_shape=jax.ShapeD...  33.7 us
    slice x1, local copies, waits for them, and re-layouts, shards(): return (out[:, :hd], out[:, hd:])  1.53 us

profile of v2, /device:TPU:0, one launch (start us, length us, event | category | flops | bytes accessed | tf_op | source)
XLA Modules:
  0.0 35.9 jit_solution(7035770142267516432)
XLA Ops:
  0.6 33.7 %shard_map.95 = bf16[256,256]{1,0:T(8,128)(2,1)} custom-call(bf16[256,128]{1,0:T(8,128)(2,1)} %q_in.1, bf16[256,128]{1,0:T(8,128)(2,1)} %qt_in.1, bf16[256,128]{1,0:T(8,128)(2,1)} %k_in.1, bf16[256,128]{1,0:T(8,128)(2,1)} %v_in.1, bf16[256,128]{1,0:T(8,128)(2,1)} %kt_in.1, bf16[256,128]{1,0:T(8,128)(2,1)} %vt_in.1, s32[8,16]{1,0:T(8,128)} %bitcast.4, ...), custom_call_target="tpu_custom_call" | custom-call | tf_op jit(solution)/shard_map/pallas_call | solution.py:292
  34.3 1.5 %fusion = (bf16[256,128]{1,0:T(8,128)(2,1)}, bf16[256,128]{1,0:T(8,128)(2,1)}) fusion(bf16[256,256]{1,0:T(8,128)(2,1)} %shard_map.95), kind=kLoop, calls=%fused_computation | loop fusion | bytes 262144 | tf_op jit(solution)/shard_map/slice | solution.py:326
